TPU v7x, 32 devices: a whole 2x2x4 slice. The times are simulated.
32 devices in a mesh: member: 2 (over x), tx: 4 (over y, core), ty: 4 (over z).
Axes of the slice: x: 2, y: 2, z: 4, core: 2. Of those that a mesh axis runs over, the one named last changes fastest.
Arguments:
- state: float32 [1024, 128, 128], P(('member', 'tx'), 'ty'), parts along dimension 0, may hold values from -6 to 6
- courant: bfloat16 [1024, 128, 128], P(('member', 'tx'), 'ty'), parts along dimension 0, may hold values from -0.3984375 to 0.3984375
- diffusion: float32 [1024, 128], P(('member', 'tx'), 'ty'), parts along dimension 0, may hold values from 0.02 to 0.2
- conv_mask: int32 [1024, 128], P(('member', 'tx'), 'ty'), parts along dimension 0, may hold values from 0 to 1, as said below
- w_in: bfloat16 [128, 1024], replicated, may hold values from -0.5 to 0.5
- w_hidden: bfloat16 [3, 1024, 1024], replicated, may hold values from -0.1875 to 0.1875
- w_out: bfloat16 [1024, 128], replicated, may hold values from -0.1875 to 0.1875
Outputs:
- state_out: float32 [1024, 128, 128], P(('member', 'tx'), 'ty'), parts along dimension 0
There are 2 independent parts, one for each index of `member`. A program takes and returns all parts, laid end to end along the dimension named above; an argument that names none is the same for every part. Nothing has to cross between parts.
Inputs may be any that keep to these rules, and one draw needn't show every extreme that they name: `conv_mask`: A tile is one device's 128 x 32 columns. A tile's used blocks are ceil(its flagged columns / 32); at most 64, reached by some tile; over a member's tiles they sum to exactly 528.
All inputs are finite; a program needn't handle non-finite values.
Results may differ from a plain program's by a relative error of at most 0.00033.
Values may be sent and summed in bfloat16 or wider, within the bound.
A program may use at most 64 MiB of HBM per device.

v0:
```python
import functools

import jax
import jax.numpy as jnp
from jax import lax
from jax.experimental import pallas as pl
from jax.experimental.pallas import tpu as pltpu
from jax.sharding import PartitionSpec as P

MESH = pl.DeviceIdType.MESH
PAD = 8
PIECES = 4
GRP = 8
ROOM = 55 << 20
TM = 1024


def advance_kernel(ntx, nty, state_hbm, courant_hbm, diffusion_ref, win_hbm, whid_hbm, wout_hbm,
                   adv_ref, win_ref, whid_ref, wout_ref, tile, wind_v, halo_n, halo_s,
                   halo_e, halo_w, coef_n, coef_s, lsem, csem, wsem, ssem, rsem):
    lon, lat, ch = wind_v.shape
    ix, iy = lax.axis_index("tx"), lax.axis_index("ty")
    east, west = lax.rem(ix + 1, ntx), lax.rem(ix + ntx - 1, ntx)
    has_n, has_s = iy < nty - 1, iy > 0
    part = lon // PIECES

    barrier = pltpu.get_barrier_semaphore()
    pl.semaphore_signal(barrier, inc=1, device_id={"tx": east}, device_id_type=MESH)
    pl.semaphore_signal(barrier, inc=1, device_id={"tx": west}, device_id_type=MESH)

    @pl.when(has_n)
    def _():
        pl.semaphore_signal(barrier, inc=1, device_id={"ty": iy + 1}, device_id_type=MESH)

    @pl.when(has_s)
    def _():
        pl.semaphore_signal(barrier, inc=1, device_id={"ty": iy - 1}, device_id_type=MESH)

    loads = []
    for k in range(PIECES):
        loads.append((
            pltpu.make_async_copy(state_hbm.at[pl.ds(k * part, part)],
                                  tile.at[pl.ds(1 + k * part, part), pl.ds(PAD, lat)], lsem.at[k]),
            pltpu.make_async_copy(courant_hbm.at[pl.ds(k * part, part)],
                                  wind_v.at[pl.ds(k * part, part)], csem.at[k])))
        for cp in loads[-1]:
            cp.start()
    weights = [pltpu.make_async_copy(src, dst, wsem.at[k]) for k, (src, dst) in enumerate(
        ((win_hbm, win_ref), (whid_hbm, whid_ref), (wout_hbm, wout_ref)))]
    for cp in weights:
        cp.start()

    @pl.when(jnp.logical_not(has_n))
    def _():
        halo_n[...] = jnp.zeros_like(halo_n)

    @pl.when(jnp.logical_not(has_s))
    def _():
        halo_s[...] = jnp.zeros_like(halo_s)

    edge = jnp.zeros((lon, 1, ch), jnp.float32)
    tile[pl.ds(1, lon), pl.ds(PAD - 1, 1), :] = edge
    tile[pl.ds(1, lon), pl.ds(PAD + lat, 1), :] = edge
    tile[pl.ds(0, 1), pl.ds(PAD, lat), :] = jnp.zeros((1, lat, ch), jnp.float32)
    tile[pl.ds(lon + 1, 1), pl.ds(PAD, lat), :] = jnp.zeros((1, lat, ch), jnp.float32)

    pl.semaphore_wait(barrier, 2 + has_n.astype(jnp.int32) + has_s.astype(jnp.int32))

    def send(src, dst, k, dev):
        return pltpu.make_async_remote_copy(
            src_ref=src, dst_ref=dst, send_sem=ssem.at[k], recv_sem=rsem.at[k],
            device_id=dev, device_id_type=MESH)

    to_n = send(state_hbm.at[:, pl.ds(lat - 1, 1)], halo_s, 2, {"ty": iy + 1})
    to_s = send(state_hbm.at[:, pl.ds(0, 1)], halo_n, 3, {"ty": iy - 1})
    to_e = send(state_hbm.at[pl.ds(lon - 1, 1)], halo_w, 0, {"tx": east})
    to_w = send(state_hbm.at[pl.ds(0, 1)], halo_e, 1, {"tx": west})
    pl.when(has_n)(to_n.start)
    pl.when(has_s)(to_s.start)
    to_e.start()
    to_w.start()

    half = ch // 2
    shape = (GRP, lat, ch)
    lane2 = lax.broadcasted_iota(jnp.int32, (GRP * lat, ch), 1)
    lane3 = lax.broadcasted_iota(jnp.int32, shape, 2)
    row3 = lax.broadcasted_iota(jnp.int32, shape, 0)

    def fields(i0):
        wind = wind_v[pl.ds(i0, GRP)].reshape(GRP * lat, ch).astype(jnp.float32) * 0.5
        turned = pltpu.roll(wind, half, 1)
        cx = jnp.where(lane2 < half, wind, turned).reshape(shape)
        cy = jnp.where(lane2 < half, turned, wind).reshape(shape)
        pick = jnp.where(lane3 == row3 + i0, diffusion_ref[...][None], 0.0)
        return cx, cy, jnp.sum(pick, axis=-1, keepdims=True)

    for k in range(PIECES):
        for piece in ([0, 1] if k == 0 else [k + 1]):
            if piece < PIECES:
                for cp in loads[piece]:
                    cp.wait()

        @pl.loop(k * part // GRP, (k + 1) * part // GRP)
        def _(c):
            i0 = pl.multiple_of(c * GRP, GRP)

            def get(di, dj):
                return tile[pl.ds(i0 + 1 + di, GRP), pl.ds(PAD + dj, lat), :]

            mid, e, w, n, s = get(0, 0), get(1, 0), get(-1, 0), get(0, 1), get(0, -1)
            cx, cy, dif = fields(i0)
            coef_n[pl.ds(i0, GRP)] = (dif - cy)[:, lat - 8:]
            coef_s[pl.ds(i0, GRP)] = (dif + cy)[:, :8]
            laplace = e + w + n + s - 4.0 * mid
            adv_ref[pl.ds(i0, GRP)] = mid - cx * (e - w) - cy * (n - s) + dif * laplace

    to_e.wait()
    to_w.wait()

    @pl.when(has_n)
    def _():
        to_n.wait_send()
        to_s.wait_recv()

    @pl.when(has_s)
    def _():
        to_s.wait_send()
        to_n.wait_recv()

    cx, _, dif = fields(0)
    adv_ref[pl.ds(0, 1)] = adv_ref[pl.ds(0, 1)] + ((dif + cx)[:1]) * halo_w[...]
    cx, _, dif = fields(lon - GRP)
    adv_ref[pl.ds(lon - 1, 1)] = adv_ref[pl.ds(lon - 1, 1)] + ((dif - cx)[GRP - 1:]) * halo_e[...]
    sub = lax.broadcasted_iota(jnp.int32, (2 * GRP, 8, ch), 1)

    @pl.loop(0, lon // (2 * GRP))
    def _(c):
        r = pl.ds(pl.multiple_of(c * 2 * GRP, 2 * GRP), 2 * GRP)
        lo, hi = pl.ds(0, 8), pl.ds(lat - 8, 8)
        adv_ref[r, lo, :] = adv_ref[r, lo, :] + jnp.where(sub == 0, coef_s[r] * halo_s[r], 0.0)
        adv_ref[r, hi, :] = adv_ref[r, hi, :] + jnp.where(sub == 7, coef_n[r] * halo_n[r], 0.0)

    for cp in weights:
        cp.wait()


def closure_kernel(mask_ref, adv, win, whid, wout, out_hbm, done, packed, ha, hb, place, base_v, base_s, bsem, osem):
    lat, lon = mask_ref.shape
    cols, ch = done.shape
    wide = GRP * lat
    chunks = cols // wide
    span = wide + 16
    layers = whid.shape[0]
    flags = mask_ref[...].astype(jnp.float32).astype(jnp.bfloat16)
    spread = (lax.broadcasted_iota(jnp.int32, (lat, wide), 1) % lat
              == lax.broadcasted_iota(jnp.int32, (lat, wide), 0)).astype(jnp.float32).astype(jnp.bfloat16)
    rep = lax.dot_general(flags, spread, (((0,), (0,)), ((), ())), preferred_element_type=jnp.float32)
    keep = (lax.broadcasted_iota(jnp.int32, (lon, wide), 1) // lat
            == lax.broadcasted_iota(jnp.int32, (lon, wide), 0) % GRP)
    rows = jnp.sum(jnp.where(keep, rep, 0.0).reshape(chunks, GRP, wide), axis=1)
    upper = (lax.broadcasted_iota(jnp.int32, (wide, wide), 0)
             < lax.broadcasted_iota(jnp.int32, (wide, wide), 1)).astype(jnp.float32).astype(jnp.bfloat16)
    rank = jnp.dot(rows.astype(jnp.bfloat16), upper, preferred_element_type=jnp.float32)
    total = jnp.sum(rows, axis=1, keepdims=True)
    lower = (lax.broadcasted_iota(jnp.int32, (chunks, chunks), 1)
             < lax.broadcasted_iota(jnp.int32, (chunks, chunks), 0)).astype(jnp.float32).astype(jnp.bfloat16)
    base = jnp.dot(lower, jnp.broadcast_to(total, (chunks, 128)).astype(jnp.bfloat16),
                   preferred_element_type=jnp.float32)
    base_i = base.astype(jnp.int32)
    base_v[...] = base_i
    cp_base = pltpu.make_async_copy(base_v, base_s, bsem)
    cp_base.start()
    rest = (base_i - (base_i // 16) * 16)[:, :1].astype(jnp.float32)
    place[...] = jnp.where(rows > 0.5, rank + rest, -1.0)
    packed[...] = jnp.zeros_like(packed)
    cp_base.wait()

    sub = lax.broadcasted_iota(jnp.int32, (span, wide), 0).astype(jnp.float32)

    def onehot(c):
        row = place[pl.ds(c, 1), :]
        return jnp.where(sub == row, 1.0, 0.0).astype(jnp.bfloat16)

    def start_of(c):
        return pl.multiple_of((base_s[c, 0] // 16) * 16, 16)

    for c in range(chunks):
        b = start_of(c)
        feats = adv[pl.ds(c * GRP, GRP)].reshape(wide, ch).astype(jnp.bfloat16)
        res = jnp.dot(onehot(c), feats, preferred_element_type=jnp.float32).astype(jnp.bfloat16)
        packed[pl.ds(b, 16), :] = packed[pl.ds(b, 16), :] + res[:16]
        packed[pl.ds(pl.multiple_of(b + 16, 16), wide), :] = res[16:]

    def silu(v):
        hv = 0.5 * v
        return (hv + hv * jnp.tanh(hv)).astype(jnp.bfloat16)

    hid = win.shape[1]
    step = 256

    @pl.loop(0, cols // 2 // TM)
    def _(t):
        r = pl.ds(pl.multiple_of(t * TM, TM), TM)
        x = packed[r, :]
        for n in range(0, hid, step):
            ha[:, n:n + step] = silu(jnp.dot(x, win[:, n:n + step], preferred_element_type=jnp.float32))
        src, dst = ha, hb
        for l in range(layers):
            for n in range(0, hid, step):
                dst[:, n:n + step] = silu(
                    jnp.dot(src[...], whid[l, :, n:n + step], preferred_element_type=jnp.float32))
            src, dst = dst, src
        packed[r, :] = jnp.dot(src[...], wout[...], preferred_element_type=jnp.float32).astype(jnp.bfloat16)

    outs = []
    for c in range(chunks):
        b = start_of(c)
        got = lax.dot_general(onehot(c), packed[pl.ds(b, span), :], (((0,), (0,)), ((), ())),
                              preferred_element_type=jnp.float32)
        r = pl.ds(c * wide, wide)
        done[r, :] = adv[pl.ds(c * GRP, GRP)].reshape(wide, ch) + got
        cp = pltpu.make_async_copy(done.at[r, :], out_hbm.at[r, :], osem.at[c])
        cp.start()
        outs.append(cp)
    for cp in outs:
        cp.wait()


def local(ntx, nty, state, courant, diffusion, conv_mask, w_in, w_hidden, w_out):
    lon, lat, ch = state.shape
    cols = lon * lat
    hid = w_in.shape[1]
    wide = GRP * lat
    chunks = cols // wide
    vmem = pl.BlockSpec(memory_space=pltpu.VMEM)
    hbm = pl.BlockSpec(memory_space=pltpu.MemorySpace.HBM)
    adv, w_in, w_hidden, w_out = pl.pallas_call(
        functools.partial(advance_kernel, ntx, nty),
        out_shape=[
            pltpu.VMEM((lon, lat, ch), jnp.float32),
            pltpu.VMEM(w_in.shape, jnp.bfloat16),
            pltpu.VMEM(w_hidden.shape, jnp.bfloat16),
            pltpu.VMEM(w_out.shape, jnp.bfloat16),
        ],
        in_specs=[hbm, hbm, vmem, hbm, hbm, hbm],
        out_specs=[vmem] * 4,
        scratch_shapes=[
            pltpu.VMEM((lon + 2, lat + 2 * PAD, ch), jnp.float32),
            pltpu.VMEM((lon, lat, ch), jnp.bfloat16),
            pltpu.VMEM((lon, 1, ch), jnp.float32),
            pltpu.VMEM((lon, 1, ch), jnp.float32),
            pltpu.VMEM((1, lat, ch), jnp.float32),
            pltpu.VMEM((1, lat, ch), jnp.float32),
            pltpu.VMEM((lon, 8, ch), jnp.float32),
            pltpu.VMEM((lon, 8, ch), jnp.float32),
            pltpu.SemaphoreType.DMA((PIECES,)),
            pltpu.SemaphoreType.DMA((PIECES,)),
            pltpu.SemaphoreType.DMA((3,)),
            pltpu.SemaphoreType.DMA((4,)),
            pltpu.SemaphoreType.DMA((4,)),
        ],
        compiler_params=pltpu.CompilerParams(collective_id=0, has_side_effects=True,
                                             vmem_limit_bytes=ROOM),
        name="advance",
    )(state, courant, diffusion.T, w_in, w_hidden, w_out)
    out = pl.pallas_call(
        closure_kernel,
        out_shape=jax.ShapeDtypeStruct((cols, ch), jnp.float32),
        in_specs=[vmem] * 5,
        out_specs=hbm,
        scratch_shapes=[
            pltpu.VMEM((cols, ch), jnp.float32),
            pltpu.VMEM((cols // 2 + wide + 32, ch), jnp.bfloat16),
            pltpu.VMEM((TM, hid), jnp.bfloat16),
            pltpu.VMEM((TM, hid), jnp.bfloat16),
            pltpu.VMEM((chunks, wide), jnp.float32),
            pltpu.VMEM((chunks, 128), jnp.int32),
            pltpu.SMEM((chunks, 128), jnp.int32),
            pltpu.SemaphoreType.DMA,
            pltpu.SemaphoreType.DMA((chunks,)),
        ],
        compiler_params=pltpu.CompilerParams(vmem_limit_bytes=ROOM // 2),
        name="closure",
    )(conv_mask.T, adv, w_in, w_hidden, w_out)
    return out.reshape(lon, lat, ch)


def solution(mesh):
    spec = P(("member", "tx"), "ty", None)
    flat = P(("member", "tx"), "ty")
    return jax.shard_map(
        functools.partial(local, mesh.shape["tx"], mesh.shape["ty"]),
        mesh=mesh,
        in_specs=(spec, spec, flat, flat, P(), P(), P()),
        out_specs=spec,
        check_vma=False,
    )
```

profile of v0, /device:TPU:0, one launch (start us, length us, event | category | flops | bytes accessed | tf_op | source)
XLA Modules:
  0.0 28.2 jit_solution(17522020113475205427)
XLA Ops:
  0.0 0.0 copy-start
  0.0 8.3 %advance.1 = (f32[128,32,128]{2,1,0:T(8,128)S(1)}, bf16[128,1024]{1,0:T(8,128)(2,1)S(1)}, bf16[3,1024,1024]{2,1,0:T(8,128)(2,1)S(1)}, bf16[1024,128]{1,0:T(8,128)(2,1)S(1)}) custom-call(f32[128,32,128]{2,1,0:T(8,128)} %state_hbm.1, bf16[128,32,128]{2,1,0:T(8,128)(2,1)} %courant_hbm.1, f32[32,128]{1,0:T(8,128)} %bitcast.4, bf16[128,1024]{1,0:T(8,128)(2,1)} %win_hbm.1, ...), custom_call_target="tpu_custom_call" | custom-call | tf_op jit(solution)/shard_map/advance/pallas_call | solution.py:237
  8.4 0.0 copy-done
  8.4 19.9 %closure.1 = f32[4096,128]{1,0:T(8,128)} custom-call(s32[32,128]{1,0:T(8,128)S(1)} %bitcast.3, f32[128,32,128]{2,1,0:T(8,128)S(1)} %get-tuple-element.9.adv, bf16[128,1024]{1,0:T(8,128)(2,1)S(1)} %get-tuple-element.10.win, bf16[3,1024,1024]{2,1,0:T(8,128)(2,1)S(1)} %get-tuple-element.11.whid, bf16[1024,128]{1,0:T(8,128)(2,1)S(1)} %get-tuple-element.12.wout), custom_call_target="tpu_custom_call" | custom-call | tf_op jit(solution)/shard_map/closure/pallas_call | solution.py:266
Async XLA Ops:
  0.0 8.4 %copy-start = (s32[128,32]{0,1:T(8,128)S(1)}, s32[128,32]{0,1:T(8,128)}, u32[]{:S(2)}) copy-start(s32[128,32]{0,1:T(8,128)} %param.10) | copy-start | bytes 49156
where the time goes:
time: 28.5 us; the launch traced here: 28.2 us
  Pallas kernels  28.2 us (99%)
    pallas_call x1, Pallas kernels, local(): pl.pallas_call(closure_kernel, out_shape=jax.ShapeDtypeStruct((cols, ch),...  19.9 us
    pallas_call x1, Pallas kernels, local(): pl.pallas_call(functools.partial(advance_kernel, ntx, nty), out_shape=[pl...  8.35 us

commit v1 on v0

v1 whole, which is shorter than its diff:
```python
import functools

import jax
import jax.numpy as jnp
from jax import lax
from jax.experimental import pallas as pl
from jax.experimental.pallas import tpu as pltpu
from jax.sharding import PartitionSpec as P

MESH = pl.DeviceIdType.MESH
PAD = 8
PIECES = 4
GRP = 8
CHUNK = 128
ROOM = 55 << 20
TM = 1024
STEP = 256


def onezero(cond):
    return cond.astype(jnp.float32).astype(jnp.bfloat16)


def iota(shape, dim):
    return lax.broadcasted_iota(jnp.int32, shape, dim)


def mm(a, b, dims=((1,), (0,))):
    return lax.dot_general(a, b, (dims, ((), ())), preferred_element_type=jnp.float32)


def advance_kernel(ntx, nty, state_hbm, courant_hbm, diffusion_ref, mask_ref, win_hbm, whid_hbm,
                   adv_ref, win_ref, whid_ref, place_ref, turned_ref, base_ref,
                   tile, wind_v, edge_n, edge_s, halo_n, halo_s, halo_e, halo_w,
                   coef_n, coef_s, coef_e, coef_w, lsem, csem, wsem, ssem, rsem):
    lon, lat, ch = wind_v.shape
    ix, iy = lax.axis_index("tx"), lax.axis_index("ty")
    east, west = lax.rem(ix + 1, ntx), lax.rem(ix + ntx - 1, ntx)
    has_n, has_s = iy < nty - 1, iy > 0
    part = lon // PIECES

    barrier = pltpu.get_barrier_semaphore()
    pl.semaphore_signal(barrier, inc=1, device_id={"tx": east}, device_id_type=MESH)
    pl.semaphore_signal(barrier, inc=1, device_id={"tx": west}, device_id_type=MESH)

    @pl.when(has_n)
    def _():
        pl.semaphore_signal(barrier, inc=1, device_id={"ty": iy + 1}, device_id_type=MESH)

    @pl.when(has_s)
    def _():
        pl.semaphore_signal(barrier, inc=1, device_id={"ty": iy - 1}, device_id_type=MESH)

    loads = [pltpu.make_async_copy(state_hbm.at[pl.ds(k * part, part)],
                                   tile.at[pl.ds(1 + k * part, part), pl.ds(PAD, lat)], lsem.at[k])
             for k in range(PIECES)]
    winds = [pltpu.make_async_copy(courant_hbm.at[pl.ds(k * part, part)],
                                   wind_v.at[pl.ds(k * part, part)], csem.at[k])
             for k in range(PIECES)]
    weights = [pltpu.make_async_copy(win_hbm, win_ref, wsem.at[0]),
               pltpu.make_async_copy(whid_hbm.at[pl.ds(0, 1)], whid_ref, wsem.at[1])]
    for cp in loads + winds + weights:
        cp.start()

    @pl.when(jnp.logical_not(has_n))
    def _():
        halo_n[...] = jnp.zeros_like(halo_n)

    @pl.when(jnp.logical_not(has_s))
    def _():
        halo_s[...] = jnp.zeros_like(halo_s)

    edge = jnp.zeros((lon, 1, ch), jnp.float32)
    tile[pl.ds(1, lon), pl.ds(PAD - 1, 1), :] = edge
    tile[pl.ds(1, lon), pl.ds(PAD + lat, 1), :] = edge
    tile[pl.ds(0, 1), pl.ds(PAD, lat), :] = jnp.zeros((1, lat, ch), jnp.float32)
    tile[pl.ds(lon + 1, 1), pl.ds(PAD, lat), :] = jnp.zeros((1, lat, ch), jnp.float32)

    per = CHUNK // lat
    chunks = lon // per
    flags = mask_ref[...].astype(jnp.float32).astype(jnp.bfloat16)
    spread = onezero(iota((lat, CHUNK), 1) % lat == iota((lat, CHUNK), 0))
    rep = mm(flags, spread, ((0,), (0,)))
    keep = iota((lon, CHUNK), 1) // lat == iota((lon, CHUNK), 0) % per
    rep = jnp.where(keep, rep, 0.0).astype(jnp.bfloat16)
    fold = onezero(iota((chunks, lon), 1) // per == iota((chunks, lon), 0))
    rows = mm(fold, rep)
    rows_b = rows.astype(jnp.bfloat16)
    first, second = iota((CHUNK, CHUNK), 0), iota((CHUNK, CHUNK), 1)
    rank = mm(rows_b, onezero(first < second))
    rank_t = mm(onezero(second < first), rows_b, ((1,), (1,)))
    rows_t = mm(onezero(first == second), rows_b, ((1,), (1,)))
    place_ref[...] = jnp.where(rows > 0.5, rank, -1.0)
    turned_ref[...] = jnp.where(rows_t > 0.5, rank_t, -1.0)
    total = jnp.broadcast_to(jnp.sum(rows, axis=1, keepdims=True), (chunks, CHUNK))
    lower = onezero(iota((chunks, chunks), 1) < iota((chunks, chunks), 0))
    base_ref[...] = mm(lower, total.astype(jnp.bfloat16)).astype(jnp.int32)

    for cp in loads:
        cp.wait()
    edge_n[...] = tile[pl.ds(1, lon), pl.ds(PAD + lat - 1, 1), :]
    edge_s[...] = tile[pl.ds(1, lon), pl.ds(PAD, 1), :]

    pl.semaphore_wait(barrier, 2 + has_n.astype(jnp.int32) + has_s.astype(jnp.int32))

    def send(src, dst, k, dev):
        return pltpu.make_async_remote_copy(
            src_ref=src, dst_ref=dst, send_sem=ssem.at[k], recv_sem=rsem.at[k],
            device_id=dev, device_id_type=MESH)

    to_n = send(edge_n, halo_s, 2, {"ty": iy + 1})
    to_s = send(edge_s, halo_n, 3, {"ty": iy - 1})
    to_e = send(state_hbm.at[pl.ds(lon - 1, 1)], halo_w, 0, {"tx": east})
    to_w = send(state_hbm.at[pl.ds(0, 1)], halo_e, 1, {"tx": west})
    pl.when(has_n)(to_n.start)
    pl.when(has_s)(to_s.start)
    to_e.start()
    to_w.start()

    half = ch // 2
    shape = (GRP, lat, ch)
    lane2 = iota((GRP * lat, ch), 1)

    def fields(i0, shift):
        wind = wind_v[pl.ds(i0, GRP)].reshape(GRP * lat, ch).astype(jnp.float32) * 0.5
        turned = pltpu.roll(wind, half, 1)
        cx = jnp.where(lane2 < half, wind, turned).reshape(shape)
        cy = jnp.where(lane2 < half, turned, wind).reshape(shape)
        near = pltpu.roll(diffusion_ref[...], shift, 1)
        dif = jnp.concatenate([jnp.broadcast_to(near[:, g:g + 1], (lat, ch))[None] for g in range(GRP)], axis=0)
        return cx, cy, dif

    for k in range(PIECES):
        winds[k].wait()

        @pl.loop(k * part // GRP, (k + 1) * part // GRP)
        def _(c):
            i0 = pl.multiple_of(c * GRP, GRP)

            def get(di, dj):
                return tile[pl.ds(i0 + 1 + di, GRP), pl.ds(PAD + dj, lat), :]

            mid, e, w, n, s = get(0, 0), get(1, 0), get(-1, 0), get(0, 1), get(0, -1)
            cx, cy, dif = fields(i0, lax.rem(lon - i0, lon))
            coef_n[pl.ds(i0, GRP)] = (dif - cy)[:, lat - 8:]
            coef_s[pl.ds(i0, GRP)] = (dif + cy)[:, :8]
            laplace = e + w + n + s - 4.0 * mid
            adv_ref[pl.ds(i0, GRP)] = mid - cx * (e - w) - cy * (n - s) + dif * laplace

    cx, _, dif = fields(0, 0)
    coef_w[...] = (dif + cx)[:1]
    cx, _, dif = fields(lon - GRP, GRP)
    coef_e[...] = (dif - cx)[GRP - 1:]

    to_e.wait()
    to_w.wait()
    adv_ref[pl.ds(0, 1)] = adv_ref[pl.ds(0, 1)] + coef_w[...] * halo_w[...]
    adv_ref[pl.ds(lon - 1, 1)] = adv_ref[pl.ds(lon - 1, 1)] + coef_e[...] * halo_e[...]

    @pl.when(has_n)
    def _():
        to_n.wait_send()
        to_s.wait_recv()

    @pl.when(has_s)
    def _():
        to_s.wait_send()
        to_n.wait_recv()

    sub = iota((2 * GRP, 8, ch), 1)

    @pl.loop(0, lon // (2 * GRP))
    def _(c):
        r = pl.ds(pl.multiple_of(c * 2 * GRP, 2 * GRP), 2 * GRP)
        lo, hi = pl.ds(0, 8), pl.ds(lat - 8, 8)
        adv_ref[r, lo, :] = adv_ref[r, lo, :] + jnp.where(sub == 0, coef_s[r] * halo_s[r], 0.0)
        adv_ref[r, hi, :] = adv_ref[r, hi, :] + jnp.where(sub == 7, coef_n[r] * halo_n[r], 0.0)

    for cp in weights:
        cp.wait()


def silu(v):
    hv = 0.5 * v
    return (hv + hv * jnp.tanh(hv)).astype(jnp.bfloat16)


def closure_kernel(adv, place, turned, base_v, win, whid0, whid_hbm, wout_hbm, out_hbm,
                   done, packed, ha, hb, whid, wout, base_s, bsem, wsem, osem):
    cols, ch = done.shape
    chunks = cols // CHUNK
    per = CHUNK // adv.shape[1]
    layers = whid.shape[0] + 1
    cp_base = pltpu.make_async_copy(base_v, base_s, bsem)
    cp_base.start()
    weights = [pltpu.make_async_copy(whid_hbm.at[pl.ds(l + 1, 1)], whid.at[pl.ds(l, 1)], wsem.at[l])
               for l in range(layers - 1)]
    weights.append(pltpu.make_async_copy(wout_hbm, wout, wsem.at[layers - 1]))
    for cp in weights:
        cp.start()
    packed[...] = jnp.zeros_like(packed)
    cp_base.wait()

    sub = iota((CHUNK, CHUNK), 0).astype(jnp.float32)
    lane = iota((CHUNK, CHUNK), 1).astype(jnp.float32)

    for c in range(chunks):
        pick = onezero(sub == place[pl.ds(c, 1), :])
        feats = adv[pl.ds(c * per, per)].reshape(CHUNK, ch).astype(jnp.bfloat16)
        packed[pl.ds(base_s[c, 0], CHUNK), :] = mm(pick, feats)

    for cp in weights:
        cp.wait()
    hid = win.shape[1]

    @pl.loop(0, cols // 2 // TM)
    def _(t):
        r = pl.ds(pl.multiple_of(t * TM, TM), TM)
        x = packed[r, :].astype(jnp.bfloat16)
        for n in range(0, hid, STEP):
            ha[:, n:n + STEP] = silu(mm(x, win[:, n:n + STEP]))
        src, dst = ha, hb
        for l in range(layers):
            w, i = (whid0, 0) if l == 0 else (whid, l - 1)
            for n in range(0, hid, STEP):
                dst[:, n:n + STEP] = silu(mm(src[...], w[i, :, n:n + STEP]))
            src, dst = dst, src
        packed[r, :] = mm(src[...], wout[...])

    outs = []
    group = 2
    for c in range(chunks):
        tend = packed[pl.ds(base_s[c, 0], CHUNK), :].astype(jnp.bfloat16)
        back = onezero(lane == turned[:, c:c + 1])
        done[pl.ds(c * CHUNK, CHUNK), :] = adv[pl.ds(c * per, per)].reshape(CHUNK, ch) + mm(back, tend)
        if c % group == group - 1:
            r = pl.ds((c + 1 - group) * CHUNK, group * CHUNK)
            cp = pltpu.make_async_copy(done.at[r, :], out_hbm.at[r, :], osem.at[c // group])
            cp.start()
            outs.append(cp)
    for cp in outs:
        cp.wait()


def local(ntx, nty, state, courant, diffusion, conv_mask, w_in, w_hidden, w_out):
    lon, lat, ch = state.shape
    cols = lon * lat
    hid = w_in.shape[1]
    layers = w_hidden.shape[0]
    chunks = cols // CHUNK
    vmem = pl.BlockSpec(memory_space=pltpu.VMEM)
    hbm = pl.BlockSpec(memory_space=pltpu.MemorySpace.HBM)
    adv, win, whid0, place, turned, base = pl.pallas_call(
        functools.partial(advance_kernel, ntx, nty),
        out_shape=[
            pltpu.VMEM((lon, lat, ch), jnp.float32),
            pltpu.VMEM(w_in.shape, jnp.bfloat16),
            pltpu.VMEM((1, hid, hid), jnp.bfloat16),
            pltpu.VMEM((chunks, CHUNK), jnp.float32),
            pltpu.VMEM((CHUNK, chunks), jnp.float32),
            pltpu.VMEM((chunks, CHUNK), jnp.int32),
        ],
        in_specs=[hbm, hbm, vmem, vmem, hbm, hbm],
        out_specs=[vmem] * 6,
        scratch_shapes=[
            pltpu.VMEM((lon + 2, lat + 2 * PAD, ch), jnp.float32),
            pltpu.VMEM((lon, lat, ch), jnp.bfloat16),
            pltpu.VMEM((lon, 1, ch), jnp.float32),
            pltpu.VMEM((lon, 1, ch), jnp.float32),
            pltpu.VMEM((lon, 1, ch), jnp.float32),
            pltpu.VMEM((lon, 1, ch), jnp.float32),
            pltpu.VMEM((1, lat, ch), jnp.float32),
            pltpu.VMEM((1, lat, ch), jnp.float32),
            pltpu.VMEM((lon, 8, ch), jnp.float32),
            pltpu.VMEM((lon, 8, ch), jnp.float32),
            pltpu.VMEM((1, lat, ch), jnp.float32),
            pltpu.VMEM((1, lat, ch), jnp.float32),
            pltpu.SemaphoreType.DMA((PIECES,)),
            pltpu.SemaphoreType.DMA((PIECES,)),
            pltpu.SemaphoreType.DMA((2,)),
            pltpu.SemaphoreType.DMA((4,)),
            pltpu.SemaphoreType.DMA((4,)),
        ],
        compiler_params=pltpu.CompilerParams(collective_id=0, has_side_effects=True,
                                             vmem_limit_bytes=ROOM),
        name="advance",
    )(state, courant, diffusion.T, conv_mask.T, w_in, w_hidden)
    out = pl.pallas_call(
        closure_kernel,
        out_shape=jax.ShapeDtypeStruct((cols, ch), jnp.float32),
        in_specs=[vmem] * 6 + [hbm] * 2,
        out_specs=hbm,
        scratch_shapes=[
            pltpu.VMEM((cols, ch), jnp.float32),
            pltpu.VMEM((cols // 2 + CHUNK, ch), jnp.float32),
            pltpu.VMEM((TM, hid), jnp.bfloat16),
            pltpu.VMEM((TM, hid), jnp.bfloat16),
            pltpu.VMEM((layers - 1, hid, hid), jnp.bfloat16),
            pltpu.VMEM(w_out.shape, jnp.bfloat16),
            pltpu.SMEM((chunks, CHUNK), jnp.int32),
            pltpu.SemaphoreType.DMA,
            pltpu.SemaphoreType.DMA((layers,)),
            pltpu.SemaphoreType.DMA((chunks,)),
        ],
        compiler_params=pltpu.CompilerParams(vmem_limit_bytes=ROOM // 2),
        name="closure",
    )(adv, place, turned, base, win, whid0, w_hidden, w_out)
    return out.reshape(lon, lat, ch)


def solution(mesh):
    spec = P(("member", "tx"), "ty", None)
    flat = P(("member", "tx"), "ty")
    return jax.shard_map(
        functools.partial(local, mesh.shape["tx"], mesh.shape["ty"]),
        mesh=mesh,
        in_specs=(spec, spec, flat, flat, P(), P(), P()),
        out_specs=spec,
        check_vma=False,
    )
```

time: 28.5 us -> 30.6 us (1.074)
  local copies, waits for them, and re-layouts: 0.01 us -> 2.78 us
  Pallas kernels: 28.2 us -> 27.6 us
    unnamed x2 -> x4, local copies, waits for them, and re-layouts: 0.01 us -> 2.78 us
    pallas_call x1, Pallas kernels: 19.9 us -> 19.2 us  [local(): pl.pallas_call(closure_kernel, out_shape=jax.ShapeDtypeStruct((cols, ch),...]
where the time goes in v1:
time: 30.6 us; the launch traced here: 30.4 us
  Pallas kernels  27.6 us (90%)
  local copies, waits for them, and re-layouts  2.78 us (9%)
    pallas_call x1, Pallas kernels, local(): pl.pallas_call(closure_kernel, out_shape=jax.ShapeDtypeStruct((cols, ch),...  19.2 us
    pallas_call x1, Pallas kernels, local(): pl.pallas_call(functools.partial(advance_kernel, ntx, nty), out_shape=[pl...  8.36 us
    unnamed x4, local copies, waits for them, and re-layouts  2.78 us

profile of v1, /device:TPU:0, one launch (start us, length us, event | category | flops | bytes accessed | tf_op | source)
XLA Modules:
  0.0 30.4 jit_solution(6635766704738170501)
XLA Ops:
  0.0 0.0 copy-start.1
  0.0 8.4 %advance.1 = (f32[128,32,128]{2,1,0:T(8,128)S(1)}, bf16[128,1024]{1,0:T(8,128)(2,1)S(1)}, bf16[1,1024,1024]{2,1,0:T(8,128)(2,1)S(1)}, f32[32,128]{1,0:T(8,128)S(...) custom-call(f32[128,32,128]{2,1,0:T(8,128)} %state_hbm.1, bf16[128,32,128]{2,1,0:T(8,128)(2,1)} %courant_hbm.1, ...), custom_call_target="tpu_custom_call" | custom-call | tf_op jit(solution)/shard_map/advance/pallas_call | solution.py:253
  8.4 0.0 copy-done.1
  8.4 0.0 copy-start
  8.4 2.8 %copy-done = bf16[3,1024,1024]{2,1,0:T(8,128)(2,1)S(1)} copy-done((bf16[3,1024,1024]{2,1,0:T(8,128)(2,1)S(1)}, bf16[3,1024,1024]{2,1,0:T(8,128)(2,1)}, u32[]{:S(2)}) %copy-start) | copy-done | bytes 6291480
  11.2 19.2 %closure.1 = f32[4096,128]{1,0:T(8,128)} custom-call(f32[128,32,128]{2,1,0:T(8,128)S(1)} %get-tuple-element.11.adv, f32[32,128]{1,0:T(8,128)S(1)} %get-tuple-element.12.place, f32[128,32]{1,0:T(8,128)S(1)} %get-tuple-element.13.turned, s32[32,128]{1,0:T(8,128)S(1)} %get-tuple-element.14.base_v, bf16[128,1024]{1,0:T(8,128)(2,1)S(1)} %get-tuple-element.15.win, ...), custom_call_target="tpu_custom_call" | custom-call | tf_op jit(solution)/shard_map/closure/pallas_call | solution.py:288
Async XLA Ops:
  0.0 8.4 %copy-start.1 = (bf16[1024,128]{1,0:T(8,128)(2,1)S(1)}, bf16[1024,128]{1,0:T(8,128)(2,1)}, u32[]{:S(2)}) copy-start(bf16[1024,128]{1,0:T(8,128)(2,1)} %wout_hbm.1) | copy-start | bytes 786436
  8.4 2.8 %copy-start = (bf16[3,1024,1024]{2,1,0:T(8,128)(2,1)S(1)}, bf16[3,1024,1024]{2,1,0:T(8,128)(2,1)}, u32[]{:S(2)}) copy-start(bf16[3,1024,1024]{2,1,0:T(8,128)(2,1)} %whid_hbm.3) | copy-start | bytes 18874372

commit v2 on v1

v2 whole, which is shorter than its diff:
```python
import functools

import jax
import jax.numpy as jnp
from jax import lax
from jax.experimental import pallas as pl
from jax.experimental.pallas import tpu as pltpu
from jax.sharding import PartitionSpec as P

MESH = pl.DeviceIdType.MESH
PAD = 8
PIECES = 4
CHUNK = 128
EDGES = 8
STEP = 256
GRANTS = (53 << 20, 41 << 20, 24 << 20)


def onezero(cond):
    return cond.astype(jnp.float32).astype(jnp.bfloat16)


def iota(shape, dim):
    return lax.broadcasted_iota(jnp.int32, shape, dim)


def mm(a, b, dims=((1,), (0,))):
    return lax.dot_general(a, b, (dims, ((), ())), preferred_element_type=jnp.float32)


def silu(v):
    hv = 0.5 * v
    return (hv + hv * jnp.tanh(hv)).astype(jnp.bfloat16)


def mlp(load, store, win, first, later, wout, ha, hb, hooks):
    hid = win.shape[1]
    x = load()
    src, dst = None, ha
    for l in range(later.shape[0] + 2):
        if l in hooks:
            hooks[l]()
        for n in range(0, hid, STEP):
            cut = slice(n, n + STEP)
            w = win[:, cut] if l == 0 else first[0, :, cut] if l == 1 else later[l - 2, :, cut]
            dst[:, cut] = silu(mm(x if l == 0 else src[...], w))
        src, dst = dst, (hb if dst is ha else ha)
    store(mm(src[...], wout[...]))


def prepare_kernel(state_hbm, courant_hbm, diffusion_hbm, mask_hbm, whid_hbm,
                   adv_ref, packed, edge_n, edge_s, edge_e, edge_w, coef_n, coef_s, coef_e, coef_w,
                   first_ref, place_ref, turned_ref, base_ref,
                   tile, wind_v, dif_v, diffusion_ref, mask_ref, base_s, lsem, csem, wsem, bsem):
    lon, lat, ch = wind_v.shape
    part = lon // PIECES
    per = CHUNK // lat
    chunks = lon // per
    tm = lon * lat // 4

    loads = [pltpu.make_async_copy(state_hbm.at[pl.ds(k * part, part)],
                                   tile.at[pl.ds(1 + k * part, part), pl.ds(PAD, lat)], lsem.at[k])
             for k in range(PIECES)]
    winds = [pltpu.make_async_copy(courant_hbm.at[pl.ds(k * part, part)],
                                   wind_v.at[pl.ds(k * part, part)], csem.at[k])
             for k in range(PIECES)]
    weight = pltpu.make_async_copy(whid_hbm.at[pl.ds(0, 1)], first_ref, wsem.at[0])
    small = [pltpu.make_async_copy(mask_hbm, mask_ref, wsem.at[1]),
             pltpu.make_async_copy(diffusion_hbm, diffusion_ref, wsem.at[2])]
    for cp in small:
        cp.start()
    for k in range(PIECES):
        loads[k].start()
        winds[k].start()
    weight.start()

    edge = jnp.zeros((lon, 1, ch), jnp.float32)
    tile[pl.ds(1, lon), pl.ds(PAD - 1, 1), :] = edge
    tile[pl.ds(1, lon), pl.ds(PAD + lat, 1), :] = edge
    tile[pl.ds(0, 1), pl.ds(PAD, lat), :] = jnp.zeros((1, lat, ch), jnp.float32)
    tile[pl.ds(lon + 1, 1), pl.ds(PAD, lat), :] = jnp.zeros((1, lat, ch), jnp.float32)
    packed[...] = jnp.zeros_like(packed)
    for cp in small:
        cp.wait()

    flags = mask_ref[...].astype(jnp.float32)
    spread = onezero(iota((lat, CHUNK), 1) % lat == iota((lat, CHUNK), 0))
    rep = mm(flags.astype(jnp.bfloat16), spread, ((0,), (0,)))
    keep = iota((lon, CHUNK), 1) // lat == iota((lon, CHUNK), 0) % per
    rep = jnp.where(keep, rep, 0.0).astype(jnp.bfloat16)
    fold = onezero(iota((chunks, lon), 1) // per == iota((chunks, lon), 0))
    rows = mm(fold, rep)
    row, col = iota((chunks, CHUNK), 0), iota((chunks, CHUNK), 1)
    rim = (col % lat == 0) | (col % lat == lat - 1)
    ends = ((row == 0) & (col < lat)) | ((row == chunks - 1) & (col >= CHUNK - lat))
    ew = jnp.sum(jnp.where(ends & jnp.logical_not(rim), rows, 0.0), axis=0, keepdims=True)
    edges = jnp.concatenate([flags[:1], flags[lat - 1:], ew, jnp.zeros((EDGES - 3, CHUNK), jnp.float32)], axis=0)
    rows = jnp.concatenate([jnp.where(rim | ends, 0.0, rows), edges], axis=0)
    rows_b = rows.astype(jnp.bfloat16)
    first, second = iota((CHUNK, CHUNK), 0), iota((CHUNK, CHUNK), 1)
    rank = mm(rows_b, onezero(first < second))
    rank_t = mm(onezero(second < first), rows_b, ((1,), (1,)))
    rows_t = mm(onezero(first == second), rows_b, ((1,), (1,)))
    place_ref[...] = jnp.where(rows > 0.5, rank, -1.0)
    turned_ref[...] = jnp.where(rows_t > 0.5, rank_t, -1.0)
    total = jnp.broadcast_to(jnp.sum(rows, axis=1, keepdims=True), rows.shape)
    both = (chunks + EDGES,) * 2
    base = mm(onezero(iota(both, 1) < iota(both, 0)), total.astype(jnp.bfloat16))
    shift = jnp.maximum(tm - base[chunks:chunks + 1], 0.0)
    base = base + jnp.where(iota(base.shape, 0) >= chunks, shift, 0.0)
    base_ref[...] = base.astype(jnp.int32)
    cp_base = pltpu.make_async_copy(base_ref, base_s, bsem)
    cp_base.start()

    for i in range(lon):
        dif_v[i] = jnp.broadcast_to(diffusion_ref[:, i:i + 1], (lat, ch))

    half = ch // 2
    lane = iota((lat, ch), 1)

    def fields(i):
        wind = wind_v[i].astype(jnp.float32)
        turned = pltpu.roll(wind, half, 1)
        cx = jnp.where(lane < half, wind, turned)
        cy = jnp.where(lane < half, turned, wind)
        return cx, cy, dif_v[i]

    sub = iota((CHUNK, CHUNK), 0).astype(jnp.float32)

    def pack(k):
        for c in range(k * part // per, (k + 1) * part // per):
            pick = onezero(sub == place_ref[pl.ds(c, 1), :])
            feats = adv_ref[pl.ds(c * per, per)].reshape(CHUNK, ch).astype(jnp.bfloat16)
            packed[pl.ds(base_s[c, 0], CHUNK), :] = mm(pick, feats)

    for k in range(PIECES):
        winds[k].wait()
        for piece in ([0, 1] if k == 0 else [k + 1]):
            if piece < PIECES:
                loads[piece].wait()
        if k == 1:
            cp_base.wait()
        for i in range(k * part, (k + 1) * part):

            def get(di, dj):
                return tile[i + 1 + di, pl.ds(PAD + dj, lat), :]

            mid, e, w, n, s = get(0, 0), get(1, 0), get(-1, 0), get(0, 1), get(0, -1)
            cx, cy, dif = fields(i)
            coef_n[i] = (dif - 0.5 * cy)[lat - 8:]
            coef_s[i] = (dif + 0.5 * cy)[:8]
            laplace = (e + w) + (n + s) - 4.0 * mid
            adv_ref[i] = mid - 0.5 * (cx * (e - w) + cy * (n - s)) + dif * laplace
        if k > 0:
            pack(k - 1)

    cx, _, dif = fields(0)
    coef_w[...] = dif + 0.5 * cx
    cx, _, dif = fields(lon - 1)
    coef_e[...] = dif - 0.5 * cx
    pitch = lat + 2 * PAD
    flat = tile.reshape((lon + 2) * pitch, ch)
    edge_n[...] = flat[pl.ds(pitch + PAD + lat - 1, lon, stride=pitch), :]
    edge_s[...] = flat[pl.ds(pitch + PAD, lon, stride=pitch), :]
    edge_e[...] = tile[lon, pl.ds(PAD, lat), :]
    edge_w[...] = tile[1, pl.ds(PAD, lat), :]
    pack(PIECES - 1)
    weight.wait()


def first_kernel(ntx, nty, packed, edge_n, edge_s, edge_e, edge_w, win, first, wout, whid_hbm,
                 tend, later, got_n, got_s, got_e, got_w,
                 ha, hb, wsem, ssem, rsem):
    ix, iy = lax.axis_index("tx"), lax.axis_index("ty")
    east, west = lax.rem(ix + 1, ntx), lax.rem(ix + ntx - 1, ntx)
    has_n, has_s = iy < nty - 1, iy > 0
    tm = ha.shape[0]

    barrier = pltpu.get_barrier_semaphore()
    pl.semaphore_signal(barrier, inc=1, device_id={"tx": east}, device_id_type=MESH)
    pl.semaphore_signal(barrier, inc=1, device_id={"tx": west}, device_id_type=MESH)

    @pl.when(has_n)
    def _():
        pl.semaphore_signal(barrier, inc=1, device_id={"ty": iy + 1}, device_id_type=MESH)

    @pl.when(has_s)
    def _():
        pl.semaphore_signal(barrier, inc=1, device_id={"ty": iy - 1}, device_id_type=MESH)

    weights = [pltpu.make_async_copy(whid_hbm.at[pl.ds(l + 1, 1)], later.at[pl.ds(l, 1)], wsem.at[l])
               for l in range(later.shape[0])]
    for cp in weights:
        cp.start()

    @pl.when(jnp.logical_not(has_n))
    def _():
        got_n[...] = jnp.zeros_like(got_n)

    @pl.when(jnp.logical_not(has_s))
    def _():
        got_s[...] = jnp.zeros_like(got_s)

    def send(src, dst, k, dev):
        return pltpu.make_async_remote_copy(
            src_ref=src, dst_ref=dst, send_sem=ssem.at[k], recv_sem=rsem.at[k],
            device_id=dev, device_id_type=MESH)

    to_n = send(edge_n, got_s, 2, {"ty": iy + 1})
    to_s = send(edge_s, got_n, 3, {"ty": iy - 1})
    to_e = send(edge_e, got_w, 0, {"tx": east})
    to_w = send(edge_w, got_e, 1, {"tx": west})

    def meet():
        pl.semaphore_wait(barrier, 2 + has_n.astype(jnp.int32) + has_s.astype(jnp.int32))
        pl.when(has_n)(to_n.start)
        pl.when(has_s)(to_s.start)
        to_e.start()
        to_w.start()

    def pause():
        for cp in weights:
            cp.wait()
        meet()

    hooks = {2: pause}

    def store(value):
        tend[...] = value

    mlp(lambda: packed[pl.ds(0, tm), :].astype(jnp.bfloat16), store, win, first, later, wout, ha, hb, hooks)

    to_e.wait()
    to_w.wait()

    @pl.when(has_n)
    def _():
        to_n.wait_send()
        to_s.wait_recv()

    @pl.when(has_s)
    def _():
        to_s.wait_send()
        to_n.wait_recv()


def second_kernel(adv, packed, head, halo_n, halo_s, halo_e, halo_w, coef_n, coef_s, coef_e, coef_w,
                  place, turned, base_v, win, first, later, wout, out_hbm,
                  done, work, tend, rim_s, rim_n, rim_ew, ha, hb, base_s, bsem, osem):
    lon, lat, ch = adv.shape
    cols = lon * lat
    chunks = cols // CHUNK
    per = CHUNK // lat
    tm = ha.shape[0]
    cp_base = pltpu.make_async_copy(base_v, base_s, bsem)
    cp_base.start()

    flat = adv.reshape(cols, ch)
    south, north = coef_s.reshape(lon * 8, ch), coef_n.reshape(lon * 8, ch)
    rim_s[...] = flat[pl.ds(0, lon, stride=lat), :] + south[pl.ds(0, lon, stride=8), :] * halo_s[...]
    rim_n[...] = flat[pl.ds(lat - 1, lon, stride=lat), :] + north[pl.ds(7, lon, stride=8), :] * halo_n[...]
    add_w, add_e = coef_w[...] * halo_w[...], coef_e[...] * halo_e[...]
    rim_s[pl.ds(0, 1), :] = rim_s[pl.ds(0, 1), :] + add_w[:1]
    rim_n[pl.ds(0, 1), :] = rim_n[pl.ds(0, 1), :] + add_w[lat - 1:]
    rim_s[pl.ds(lon - 1, 1), :] = rim_s[pl.ds(lon - 1, 1), :] + add_e[:1]
    rim_n[pl.ds(lon - 1, 1), :] = rim_n[pl.ds(lon - 1, 1), :] + add_e[lat - 1:]
    rim_ew[...] = jnp.zeros_like(rim_ew)
    rim_ew[pl.ds(0, lat), :] = adv[0] + add_w
    rim_ew[pl.ds(CHUNK - lat, lat), :] = adv[lon - 1] + add_e

    work[...] = packed[pl.ds(tm, tm + CHUNK), :]
    tend[pl.ds(0, tm), :] = head[...]
    tend[pl.ds(2 * tm, CHUNK), :] = jnp.zeros((CHUNK, ch), jnp.float32)
    cp_base.wait()

    sub = iota((CHUNK, CHUNK), 0).astype(jnp.float32)
    lane = iota((CHUNK, CHUNK), 1).astype(jnp.float32)
    rims = (rim_s, rim_n, rim_ew)
    for k, rim in enumerate(rims):
        pick = onezero(sub == place[pl.ds(chunks + k, 1), :])
        work[pl.ds(base_s[chunks + k, 0] - tm, CHUNK), :] = mm(pick, rim[...].astype(jnp.bfloat16))

    def store(value):
        tend[pl.ds(tm, tm), :] = value

    mlp(lambda: work[pl.ds(0, tm), :].astype(jnp.bfloat16), store, win, first, later, wout, ha, hb, {})

    def spread(c):
        rows = tend[pl.ds(base_s[c, 0], CHUNK), :].astype(jnp.bfloat16)
        return mm(onezero(lane == turned[:, c:c + 1]), rows)

    for k, rim in enumerate(rims):
        rim[...] = rim[...] + spread(chunks + k)

    outs = []
    group = 2
    for c in range(chunks):
        done[pl.ds(c * CHUNK, CHUNK), :] = flat[pl.ds(c * CHUNK, CHUNK), :] + spread(c)
        if c == 0:
            done[pl.ds(0, lat), :] = rim_ew[pl.ds(0, lat), :]
        if c == chunks - 1:
            done[pl.ds(cols - lat, lat), :] = rim_ew[pl.ds(CHUNK - lat, lat), :]
        for i in range(c * per, (c + 1) * per):
            done[pl.ds(i * lat, 1), :] = rim_s[pl.ds(i, 1), :]
            done[pl.ds(i * lat + lat - 1, 1), :] = rim_n[pl.ds(i, 1), :]
        if c % group == group - 1:
            r = pl.ds((c + 1 - group) * CHUNK, group * CHUNK)
            cp = pltpu.make_async_copy(done.at[r, :], out_hbm.at[r, :], osem.at[c // group])
            cp.start()
            outs.append(cp)
    for cp in outs:
        cp.wait()


def local(ntx, nty, state, courant, diffusion, conv_mask, w_in, w_hidden, w_out):
    lon, lat, ch = state.shape
    assert lon == CHUNK
    cols = lon * lat
    hid = w_in.shape[1]
    layers = w_hidden.shape[0]
    chunks = cols // CHUNK
    tm = cols // 4
    f32, bf16 = jnp.float32, jnp.bfloat16
    vmem = pl.BlockSpec(memory_space=pltpu.VMEM)
    hbm = pl.BlockSpec(memory_space=pltpu.MemorySpace.HBM)
    (adv, packed, edge_n, edge_s, edge_e, edge_w, coef_n, coef_s, coef_e, coef_w,
     first, place, turned, base) = pl.pallas_call(
        prepare_kernel,
        out_shape=[
            pltpu.VMEM((lon, lat, ch), f32),
            pltpu.VMEM((2 * tm + CHUNK, ch), f32),
            pltpu.VMEM((lon, ch), f32),
            pltpu.VMEM((lon, ch), f32),
            pltpu.VMEM((lat, ch), f32),
            pltpu.VMEM((lat, ch), f32),
            pltpu.VMEM((lon, 8, ch), f32),
            pltpu.VMEM((lon, 8, ch), f32),
            pltpu.VMEM((lat, ch), f32),
            pltpu.VMEM((lat, ch), f32),
            pltpu.VMEM((1, hid, hid), bf16),
            pltpu.VMEM((chunks + EDGES, CHUNK), f32),
            pltpu.VMEM((CHUNK, chunks + EDGES), f32),
            pltpu.VMEM((chunks + EDGES, CHUNK), jnp.int32),
        ],
        in_specs=[hbm] * 5,
        out_specs=[vmem] * 14,
        scratch_shapes=[
            pltpu.VMEM((lon + 2, lat + 2 * PAD, ch), f32),
            pltpu.VMEM((lon, lat, ch), bf16),
            pltpu.VMEM((lon, lat, ch), f32),
            pltpu.VMEM((lat, lon), f32),
            pltpu.VMEM((lat, lon), jnp.int32),
            pltpu.SMEM((chunks + EDGES, CHUNK), jnp.int32),
            pltpu.SemaphoreType.DMA((PIECES,)),
            pltpu.SemaphoreType.DMA((PIECES,)),
            pltpu.SemaphoreType.DMA((3,)),
            pltpu.SemaphoreType.DMA,
        ],
        compiler_params=pltpu.CompilerParams(vmem_limit_bytes=GRANTS[0]),
        name="prepare",
    )(state, courant, diffusion.T, conv_mask.T, w_hidden)
    head, later, halo_n, halo_s, halo_e, halo_w = pl.pallas_call(
        functools.partial(first_kernel, ntx, nty),
        out_shape=[
            pltpu.VMEM((tm, ch), f32),
            pltpu.VMEM((layers - 1, hid, hid), bf16),
            pltpu.VMEM((lon, ch), f32),
            pltpu.VMEM((lon, ch), f32),
            pltpu.VMEM((lat, ch), f32),
            pltpu.VMEM((lat, ch), f32),
        ],
        in_specs=[vmem] * 8 + [hbm],
        out_specs=[vmem] * 6,
        scratch_shapes=[
            pltpu.VMEM((tm, hid), bf16),
            pltpu.VMEM((tm, hid), bf16),
            pltpu.SemaphoreType.DMA((layers - 1,)),
            pltpu.SemaphoreType.DMA((4,)),
            pltpu.SemaphoreType.DMA((4,)),
        ],
        compiler_params=pltpu.CompilerParams(collective_id=0, has_side_effects=True,
                                             vmem_limit_bytes=GRANTS[1]),
        name="first",
    )(packed, edge_n, edge_s, edge_e, edge_w, w_in, first, w_out, w_hidden)
    out = pl.pallas_call(
        second_kernel,
        out_shape=jax.ShapeDtypeStruct((cols, ch), f32),
        in_specs=[vmem] * 18,
        out_specs=hbm,
        scratch_shapes=[
            pltpu.VMEM((cols, ch), f32),
            pltpu.VMEM((tm + CHUNK, ch), f32),
            pltpu.VMEM((2 * tm + CHUNK, ch), f32),
            pltpu.VMEM((lon, ch), f32),
            pltpu.VMEM((lon, ch), f32),
            pltpu.VMEM((CHUNK, ch), f32),
            pltpu.VMEM((tm, hid), bf16),
            pltpu.VMEM((tm, hid), bf16),
            pltpu.SMEM((chunks + EDGES, CHUNK), jnp.int32),
            pltpu.SemaphoreType.DMA,
            pltpu.SemaphoreType.DMA((chunks,)),
        ],
        compiler_params=pltpu.CompilerParams(vmem_limit_bytes=GRANTS[2]),
        name="second",
    )(adv, packed, head, halo_n, halo_s, halo_e, halo_w, coef_n, coef_s, coef_e, coef_w,
      place, turned, base, w_in, first, later, w_out)
    return out.reshape(lon, lat, ch)


def solution(mesh):
    spec = P(("member", "tx"), "ty", None)
    flat = P(("member", "tx"), "ty")
    return jax.shard_map(
        functools.partial(local, mesh.shape["tx"], mesh.shape["ty"]),
        mesh=mesh,
        in_specs=(spec, spec, flat, flat, P(), P(), P()),
        out_specs=spec,
        check_vma=False,
    )
```

time: 30.6 us -> 26.6 us (0.87)
  local copies, waits for them, and re-layouts: 2.78 us -> 0.01 us
  Pallas kernels: 27.6 us -> 26.2 us
    unnamed x4, local copies, waits for them, and re-layouts: 2.78 us -> 0.01 us
    pallas_call x2 -> x3, Pallas kernels: 27.6 us -> 26.2 us  [the longest x1 11.4 us: local(): pl.pallas_call(second_kernel, out_shape=jax.ShapeDtypeStruct((cols, ch),...]
where the time goes in v2:
time: 26.6 us; the launch traced here: 26.4 us
  Pallas kernels  26.2 us (98%)
    pallas_call x1, Pallas kernels, local(): pl.pallas_call(second_kernel, out_shape=jax.ShapeDtypeStruct((cols, ch),...  11.4 us
    pallas_call x1, Pallas kernels, local(): pl.pallas_call(functools.partial(first_kernel, ntx, nty), out_shape=[pltp...  10.1 us
    pallas_call x1, Pallas kernels, local(): pl.pallas_call(prepare_kernel, out_shape=[pltpu.VMEM((lon, lat, ch), f32)...  4.72 us

profile of v2, /device:TPU:0, one launch (start us, length us, event | category | flops | bytes accessed | tf_op | source)
XLA Modules:
  0.0 26.4 jit_solution(6955621721346804631)
XLA Ops:
  0.0 0.0 copy-start
  0.0 0.0 copy-start.1
  0.0 4.7 %prepare.1 = (f32[128,32,128]{2,1,0:T(8,128)S(1)}, f32[2176,128]{1,0:T(8,128)S(1)}, f32[128,128]{1,0:T(8,128)S(1)}, f32[128,128]{1,0:T(8,128)S(1)}, f32[32,128]{...) custom-call(f32[128,32,128]{2,1,0:T(8,128)} %state_hbm.1, ...), custom_call_target="tpu_custom_call" | custom-call | tf_op jit(solution)/shard_map/prepare/pallas_call | solution.py:327
  4.7 0.0 copy-done
  4.7 0.0 copy-done.1
  4.8 10.1 %first.1 = (f32[1024,128]{1,0:T(8,128)S(1)}, bf16[2,1024,1024]{2,1,0:T(8,128)(2,1)S(1)}, f32[128,128]{1,0:T(8,128)S(1)}, f32[128,128]{1,0:T(8,128)S(1)}, f32[32,128]{1,0:T(8,128)S(1)}, /*index=5*/f32[32,128]{1,0:T(8,128)S(1)}) custom-call(f32[2176,128]{1,0:T(8,128)S(1)} %get-tuple-element.26.packed, f32[128,128]{1,0:T(8,128)S(1)} %get-tuple-element.27.edge_n, ...), custom_call_target="tpu_custom_call" | custom-call | tf_op jit(solution)/shard_map/first/pallas_call | solution.py:362
  14.9 11.4 %second.1 = f32[4096,128]{1,0:T(8,128)} custom-call(f32[128,32,128]{2,1,0:T(8,128)S(1)} %get-tuple-element.25.adv, f32[2176,128]{1,0:T(8,128)S(1)} %get-tuple-element.26.packed, f32[1024,128]{1,0:T(8,128)S(1)} %get-tuple-element.32.head, f32[128,128]{1,0:T(8,128)S(1)} %get-tuple-element.33.halo_n, f32[128,128]{1,0:T(8,128)S(1)} %get-tuple-element.34.halo_s, ...), custom_call_target="tpu_custom_call" | custom-call | tf_op jit(solution)/shard_map/second/pallas_call | solution.py:385
Async XLA Ops:
  0.0 4.7 %copy-start = (bf16[128,1024]{1,0:T(8,128)(2,1)S(1)}, bf16[128,1024]{1,0:T(8,128)(2,1)}, u32[]{:S(2)}) copy-start(bf16[128,1024]{1,0:T(8,128)(2,1)} %win.3) | copy-start | bytes 786436
  0.0 4.7 %copy-start.1 = (bf16[1024,128]{1,0:T(8,128)(2,1)S(1)}, bf16[1024,128]{1,0:T(8,128)(2,1)}, u32[]{:S(2)}) copy-start(bf16[1024,128]{1,0:T(8,128)(2,1)} %wout.3) | copy-start | bytes 786436

commit v3 on v2

--- a/solution.py
+++ b/solution.py
@@ -13,7 +13,7 @@
 CHUNK = 128
 EDGES = 8
 STEP = 256
-GRANTS = (53 << 20, 41 << 20, 24 << 20)
+GRANTS = (50 << 20, 24 << 20, 24 << 20)
 
 
 def onezero(cond):
@@ -33,16 +33,14 @@
     return (hv + hv * jnp.tanh(hv)).astype(jnp.bfloat16)
 
 
-def mlp(load, store, win, first, later, wout, ha, hb, hooks):
+def mlp(load, store, win, whid, wout, ha, hb):
     hid = win.shape[1]
     x = load()
     src, dst = None, ha
-    for l in range(later.shape[0] + 2):
-        if l in hooks:
-            hooks[l]()
+    for l in range(whid.shape[0] + 1):
         for n in range(0, hid, STEP):
             cut = slice(n, n + STEP)
-            w = win[:, cut] if l == 0 else first[0, :, cut] if l == 1 else later[l - 2, :, cut]
+            w = win[:, cut] if l == 0 else whid[l - 1, :, cut]
             dst[:, cut] = silu(mm(x if l == 0 else src[...], w))
         src, dst = dst, (hb if dst is ha else ha)
     store(mm(src[...], wout[...]))
@@ -50,7 +48,7 @@
 
 def prepare_kernel(state_hbm, courant_hbm, diffusion_hbm, mask_hbm, whid_hbm,
                    adv_ref, packed, edge_n, edge_s, edge_e, edge_w, coef_n, coef_s, coef_e, coef_w,
-                   first_ref, place_ref, turned_ref, base_ref,
+                   whid_ref, place_ref, turned_ref, base_ref,
                    tile, wind_v, dif_v, diffusion_ref, mask_ref, base_s, lsem, csem, wsem, bsem):
     lon, lat, ch = wind_v.shape
     part = lon // PIECES
@@ -64,7 +62,7 @@
     winds = [pltpu.make_async_copy(courant_hbm.at[pl.ds(k * part, part)],
                                    wind_v.at[pl.ds(k * part, part)], csem.at[k])
              for k in range(PIECES)]
-    weight = pltpu.make_async_copy(whid_hbm.at[pl.ds(0, 1)], first_ref, wsem.at[0])
+    weight = pltpu.make_async_copy(whid_hbm, whid_ref, wsem.at[0])
     small = [pltpu.make_async_copy(mask_hbm, mask_ref, wsem.at[1]),
              pltpu.make_async_copy(diffusion_hbm, diffusion_ref, wsem.at[2])]
     for cp in small:
@@ -168,9 +166,9 @@
     weight.wait()
 
 
-def first_kernel(ntx, nty, packed, edge_n, edge_s, edge_e, edge_w, win, first, wout, whid_hbm,
-                 tend, later, got_n, got_s, got_e, got_w,
-                 ha, hb, wsem, ssem, rsem):
+def first_kernel(ntx, nty, packed, edge_n, edge_s, edge_e, edge_w, win, whid, wout,
+                 tend, got_n, got_s, got_e, got_w,
+                 ha, hb, ssem, rsem):
     ix, iy = lax.axis_index("tx"), lax.axis_index("ty")
     east, west = lax.rem(ix + 1, ntx), lax.rem(ix + ntx - 1, ntx)
     has_n, has_s = iy < nty - 1, iy > 0
@@ -187,11 +185,6 @@
     @pl.when(has_s)
     def _():
         pl.semaphore_signal(barrier, inc=1, device_id={"ty": iy - 1}, device_id_type=MESH)
-
-    weights = [pltpu.make_async_copy(whid_hbm.at[pl.ds(l + 1, 1)], later.at[pl.ds(l, 1)], wsem.at[l])
-               for l in range(later.shape[0])]
-    for cp in weights:
-        cp.start()
 
     @pl.when(jnp.logical_not(has_n))
     def _():
@@ -218,17 +211,17 @@
         to_e.start()
         to_w.start()
 
-    def pause():
-        for cp in weights:
-            cp.wait()
-        meet()
-
-    hooks = {2: pause}
-
-    def store(value):
-        tend[...] = value
-
-    mlp(lambda: packed[pl.ds(0, tm), :].astype(jnp.bfloat16), store, win, first, later, wout, ha, hb, hooks)
+    def tile(at, size):
+        r = pl.ds(at, size)
+
+        def store(value):
+            tend[r, :] = value
+
+        mlp(lambda: packed[r, :].astype(jnp.bfloat16), store, win, whid, wout, ha.at[r], hb.at[r])
+
+    tile(0, tm // 4)
+    meet()
+    tile(tm // 4, tm - tm // 4)
 
     to_e.wait()
     to_w.wait()
@@ -245,7 +238,7 @@
 
 
 def second_kernel(adv, packed, head, halo_n, halo_s, halo_e, halo_w, coef_n, coef_s, coef_e, coef_w,
-                  place, turned, base_v, win, first, later, wout, out_hbm,
+                  place, turned, base_v, win, whid, wout, out_hbm,
                   done, work, tend, rim_s, rim_n, rim_ew, ha, hb, base_s, bsem, osem):
     lon, lat, ch = adv.shape
     cols = lon * lat
@@ -283,7 +276,7 @@
     def store(value):
         tend[pl.ds(tm, tm), :] = value
 
-    mlp(lambda: work[pl.ds(0, tm), :].astype(jnp.bfloat16), store, win, first, later, wout, ha, hb, {})
+    mlp(lambda: work[pl.ds(0, tm), :].astype(jnp.bfloat16), store, win, whid, wout, ha, hb)
 
     def spread(c):
         rows = tend[pl.ds(base_s[c, 0], CHUNK), :].astype(jnp.bfloat16)
@@ -317,14 +310,13 @@
     assert lon == CHUNK
     cols = lon * lat
     hid = w_in.shape[1]
-    layers = w_hidden.shape[0]
     chunks = cols // CHUNK
     tm = cols // 4
     f32, bf16 = jnp.float32, jnp.bfloat16
     vmem = pl.BlockSpec(memory_space=pltpu.VMEM)
     hbm = pl.BlockSpec(memory_space=pltpu.MemorySpace.HBM)
     (adv, packed, edge_n, edge_s, edge_e, edge_w, coef_n, coef_s, coef_e, coef_w,
-     first, place, turned, base) = pl.pallas_call(
+     whid, place, turned, base) = pl.pallas_call(
         prepare_kernel,
         out_shape=[
             pltpu.VMEM((lon, lat, ch), f32),
@@ -337,7 +329,7 @@
             pltpu.VMEM((lon, 8, ch), f32),
             pltpu.VMEM((lat, ch), f32),
             pltpu.VMEM((lat, ch), f32),
-            pltpu.VMEM((1, hid, hid), bf16),
+            pltpu.VMEM(w_hidden.shape, bf16),
             pltpu.VMEM((chunks + EDGES, CHUNK), f32),
             pltpu.VMEM((CHUNK, chunks + EDGES), f32),
             pltpu.VMEM((chunks + EDGES, CHUNK), jnp.int32),
@@ -359,33 +351,31 @@
         compiler_params=pltpu.CompilerParams(vmem_limit_bytes=GRANTS[0]),
         name="prepare",
     )(state, courant, diffusion.T, conv_mask.T, w_hidden)
-    head, later, halo_n, halo_s, halo_e, halo_w = pl.pallas_call(
+    head, halo_n, halo_s, halo_e, halo_w = pl.pallas_call(
         functools.partial(first_kernel, ntx, nty),
         out_shape=[
             pltpu.VMEM((tm, ch), f32),
-            pltpu.VMEM((layers - 1, hid, hid), bf16),
             pltpu.VMEM((lon, ch), f32),
             pltpu.VMEM((lon, ch), f32),
             pltpu.VMEM((lat, ch), f32),
             pltpu.VMEM((lat, ch), f32),
         ],
-        in_specs=[vmem] * 8 + [hbm],
-        out_specs=[vmem] * 6,
+        in_specs=[vmem] * 8,
+        out_specs=[vmem] * 5,
         scratch_shapes=[
             pltpu.VMEM((tm, hid), bf16),
             pltpu.VMEM((tm, hid), bf16),
-            pltpu.SemaphoreType.DMA((layers - 1,)),
             pltpu.SemaphoreType.DMA((4,)),
             pltpu.SemaphoreType.DMA((4,)),
         ],
         compiler_params=pltpu.CompilerParams(collective_id=0, has_side_effects=True,
                                              vmem_limit_bytes=GRANTS[1]),
         name="first",
-    )(packed, edge_n, edge_s, edge_e, edge_w, w_in, first, w_out, w_hidden)
+    )(packed, edge_n, edge_s, edge_e, edge_w, w_in, whid, w_out)
     out = pl.pallas_call(
         second_kernel,
         out_shape=jax.ShapeDtypeStruct((cols, ch), f32),
-        in_specs=[vmem] * 18,
+        in_specs=[vmem] * 17,
         out_specs=hbm,
         scratch_shapes=[
             pltpu.VMEM((cols, ch), f32),
@@ -403,7 +393,7 @@
         compiler_params=pltpu.CompilerParams(vmem_limit_bytes=GRANTS[2]),
         name="second",
     )(adv, packed, head, halo_n, halo_s, halo_e, halo_w, coef_n, coef_s, coef_e, coef_w,
-      place, turned, base, w_in, first, later, w_out)
+      place, turned, base, w_in, whid, w_out)
     return out.reshape(lon, lat, ch)
 
 

time: 26.6 us -> 25.8 us (0.970)
  Pallas kernels: 26.2 us -> 25.4 us
    pallas_call x1, Pallas kernels: 10.1 us -> 9.34 us  [local(): pl.pallas_call(functools.partial(first_kernel, ntx, nty), out_shape=[pltp...]
where the time goes in v3:
time: 25.8 us; the launch traced here: 25.6 us
  Pallas kernels  25.4 us (98%)
    pallas_call x1, Pallas kernels, local(): pl.pallas_call(second_kernel, out_shape=jax.ShapeDtypeStruct((cols, ch),...  11.3 us
    pallas_call x1, Pallas kernels, local(): pl.pallas_call(functools.partial(first_kernel, ntx, nty), out_shape=[pltp...  9.34 us
    pallas_call x1, Pallas kernels, local(): pl.pallas_call(prepare_kernel, out_shape=[pltpu.VMEM((lon, lat, ch), f32)...  4.72 us

profile of v3, /device:TPU:0, one launch (start us, length us, event | category | flops | bytes accessed | tf_op | source)
XLA Modules:
  0.0 25.6 jit_solution(13933323325893055635)
XLA Ops:
  0.0 0.0 copy-start
  0.0 0.0 copy-start.1
  0.0 4.7 %prepare.1 = (f32[128,32,128]{2,1,0:T(8,128)S(1)}, f32[2176,128]{1,0:T(8,128)S(1)}, f32[128,128]{1,0:T(8,128)S(1)}, f32[128,128]{1,0:T(8,128)S(1)}, f32[32,128]{...) custom-call(f32[128,32,128]{2,1,0:T(8,128)} %state_hbm.1, ...), custom_call_target="tpu_custom_call" | custom-call | tf_op jit(solution)/shard_map/prepare/pallas_call | solution.py:319
  4.7 0.0 copy-done
  4.7 0.0 copy-done.1
  4.8 9.3 %first.1 = (f32[1024,128]{1,0:T(8,128)S(1)}, f32[128,128]{1,0:T(8,128)S(1)}, f32[128,128]{1,0:T(8,128)S(1)}, f32[32,128]{1,0:T(8,128)S(1)}, f32[32,128]{1,0:T(8,128)S(1)}) custom-call(f32[2176,128]{1,0:T(8,128)S(1)} %get-tuple-element.25.packed, f32[128,128]{1,0:T(8,128)S(1)} %get-tuple-element.26.edge_n, f32[128,128]{1,0:T(8,128)S(1)} %get-tuple-element.27.edge_s, ...), custom_call_target="tpu_custom_call" | custom-call | tf_op jit(solution)/shard_map/first/pallas_call | solution.py:354
  14.1 11.3 %second.1 = f32[4096,128]{1,0:T(8,128)} custom-call(f32[128,32,128]{2,1,0:T(8,128)S(1)} %get-tuple-element.24.adv, f32[2176,128]{1,0:T(8,128)S(1)} %get-tuple-element.25.packed, f32[1024,128]{1,0:T(8,128)S(1)} %get-tuple-element.31.head, f32[128,128]{1,0:T(8,128)S(1)} %get-tuple-element.32.halo_n, f32[128,128]{1,0:T(8,128)S(1)} %get-tuple-element.33.halo_s, ...), custom_call_target="tpu_custom_call" | custom-call | tf_op jit(solution)/shard_map/second/pallas_call | solution.py:375
Async XLA Ops:
  0.0 4.7 %copy-start = (bf16[128,1024]{1,0:T(8,128)(2,1)S(1)}, bf16[128,1024]{1,0:T(8,128)(2,1)}, u32[]{:S(2)}) copy-start(bf16[128,1024]{1,0:T(8,128)(2,1)} %win.3) | copy-start | bytes 786436
  0.0 4.7 %copy-start.1 = (bf16[1024,128]{1,0:T(8,128)(2,1)S(1)}, bf16[1024,128]{1,0:T(8,128)(2,1)}, u32[]{:S(2)}) copy-start(bf16[1024,128]{1,0:T(8,128)(2,1)} %wout.3) | copy-start | bytes 786436

commit v4 on v3

--- a/solution.py
+++ b/solution.py
@@ -136,7 +136,7 @@
         for piece in ([0, 1] if k == 0 else [k + 1]):
             if piece < PIECES:
                 loads[piece].wait()
-        if k == 1:
+        if k == PIECES - 1:
             cp_base.wait()
         for i in range(k * part, (k + 1) * part):
 
@@ -149,8 +149,9 @@
             coef_s[i] = (dif + 0.5 * cy)[:8]
             laplace = (e + w) + (n + s) - 4.0 * mid
             adv_ref[i] = mid - 0.5 * (cx * (e - w) + cy * (n - s)) + dif * laplace
-        if k > 0:
-            pack(k - 1)
+        if k == PIECES - 1:
+            for early in range(k):
+                pack(early)
 
     cx, _, dif = fields(0)
     coef_w[...] = dif + 0.5 * cx
@@ -264,19 +265,21 @@
     work[...] = packed[pl.ds(tm, tm + CHUNK), :]
     tend[pl.ds(0, tm), :] = head[...]
     tend[pl.ds(2 * tm, CHUNK), :] = jnp.zeros((CHUNK, ch), jnp.float32)
-    cp_base.wait()
 
     sub = iota((CHUNK, CHUNK), 0).astype(jnp.float32)
     lane = iota((CHUNK, CHUNK), 1).astype(jnp.float32)
     rims = (rim_s, rim_n, rim_ew)
     for k, rim in enumerate(rims):
         pick = onezero(sub == place[pl.ds(chunks + k, 1), :])
-        work[pl.ds(base_s[chunks + k, 0] - tm, CHUNK), :] = mm(pick, rim[...].astype(jnp.bfloat16))
+        at = jnp.max(base_v[pl.ds(chunks + k, 1), :].astype(jnp.float32)).astype(jnp.int32)
+        work[pl.ds(at - tm, CHUNK), :] = mm(pick, rim[...].astype(jnp.bfloat16))
 
     def store(value):
         tend[pl.ds(tm, tm), :] = value
 
     mlp(lambda: work[pl.ds(0, tm), :].astype(jnp.bfloat16), store, win, whid, wout, ha, hb)
+
+    cp_base.wait()
 
     def spread(c):
         rows = tend[pl.ds(base_s[c, 0], CHUNK), :].astype(jnp.bfloat16)

time: 25.8 us -> 24.6 us (0.953)
  Pallas kernels: 25.4 us -> 24.2 us
    pallas_call x1, Pallas kernels: 11.3 us -> 10.6 us  [local(): pl.pallas_call(second_kernel, out_shape=jax.ShapeDtypeStruct((cols, ch),...]
    pallas_call x1, Pallas kernels: 4.72 us -> 4.3 us  [local(): pl.pallas_call(prepare_kernel, out_shape=[pltpu.VMEM((lon, lat, ch), f32)...]
where the time goes in v4:
time: 24.6 us; the launch traced here: 24.5 us
  Pallas kernels  24.2 us (98%)
    pallas_call x1, Pallas kernels, local(): pl.pallas_call(second_kernel, out_shape=jax.ShapeDtypeStruct((cols, ch),...  10.6 us
    pallas_call x1, Pallas kernels, local(): pl.pallas_call(functools.partial(first_kernel, ntx, nty), out_shape=[pltp...  9.34 us
    pallas_call x1, Pallas kernels, local(): pl.pallas_call(prepare_kernel, out_shape=[pltpu.VMEM((lon, lat, ch), f32)...  4.3 us

profile of v4, /device:TPU:0, one launch (start us, length us, event | category | flops | bytes accessed | tf_op | source)
XLA Modules:
  0.0 24.5 jit_solution(1090436273711891911)
XLA Ops:
  0.0 0.0 copy-start
  0.0 0.0 copy-start.1
  0.0 4.3 %prepare.1 = (f32[128,32,128]{2,1,0:T(8,128)S(1)}, f32[2176,128]{1,0:T(8,128)S(1)}, f32[128,128]{1,0:T(8,128)S(1)}, f32[128,128]{1,0:T(8,128)S(1)}, f32[32,128]{...) custom-call(f32[128,32,128]{2,1,0:T(8,128)} %state_hbm.1, ...), custom_call_target="tpu_custom_call" | custom-call | tf_op jit(solution)/shard_map/prepare/pallas_call | solution.py:322
  4.3 0.0 copy-done
  4.3 0.0 copy-done.1
  4.3 9.3 %first.1 = (f32[1024,128]{1,0:T(8,128)S(1)}, f32[128,128]{1,0:T(8,128)S(1)}, f32[128,128]{1,0:T(8,128)S(1)}, f32[32,128]{1,0:T(8,128)S(1)}, f32[32,128]{1,0:T(8,128)S(1)}) custom-call(f32[2176,128]{1,0:T(8,128)S(1)} %get-tuple-element.25.packed, f32[128,128]{1,0:T(8,128)S(1)} %get-tuple-element.26.edge_n, f32[128,128]{1,0:T(8,128)S(1)} %get-tuple-element.27.edge_s, ...), custom_call_target="tpu_custom_call" | custom-call | tf_op jit(solution)/shard_map/first/pallas_call | solution.py:357
  13.7 10.6 %second.1 = f32[4096,128]{1,0:T(8,128)} custom-call(f32[128,32,128]{2,1,0:T(8,128)S(1)} %get-tuple-element.24.adv, f32[2176,128]{1,0:T(8,128)S(1)} %get-tuple-element.25.packed, f32[1024,128]{1,0:T(8,128)S(1)} %get-tuple-element.31.head, f32[128,128]{1,0:T(8,128)S(1)} %get-tuple-element.32.halo_n, f32[128,128]{1,0:T(8,128)S(1)} %get-tuple-element.33.halo_s, ...), custom_call_target="tpu_custom_call" | custom-call | tf_op jit(solution)/shard_map/second/pallas_call | solution.py:378
Async XLA Ops:
  0.0 4.3 %copy-start = (bf16[128,1024]{1,0:T(8,128)(2,1)S(1)}, bf16[128,1024]{1,0:T(8,128)(2,1)}, u32[]{:S(2)}) copy-start(bf16[128,1024]{1,0:T(8,128)(2,1)} %win.3) | copy-start | bytes 786436
  0.0 4.3 %copy-start.1 = (bf16[1024,128]{1,0:T(8,128)(2,1)S(1)}, bf16[1024,128]{1,0:T(8,128)(2,1)}, u32[]{:S(2)}) copy-start(bf16[1024,128]{1,0:T(8,128)(2,1)} %wout.3) | copy-start | bytes 786436

commit v5 on v4

--- a/solution.py
+++ b/solution.py
@@ -240,7 +240,7 @@
 
 def second_kernel(adv, packed, head, halo_n, halo_s, halo_e, halo_w, coef_n, coef_s, coef_e, coef_w,
                   place, turned, base_v, win, whid, wout, out_hbm,
-                  done, work, tend, rim_s, rim_n, rim_ew, ha, hb, base_s, bsem, osem):
+                  done, work, tend, back, rim_s, rim_n, rim_ew, ha, hb, base_s, bsem, osem):
     lon, lat, ch = adv.shape
     cols = lon * lat
     chunks = cols // CHUNK
@@ -274,6 +274,9 @@
         at = jnp.max(base_v[pl.ds(chunks + k, 1), :].astype(jnp.float32)).astype(jnp.int32)
         work[pl.ds(at - tm, CHUNK), :] = mm(pick, rim[...].astype(jnp.bfloat16))
 
+    for c in range(chunks + len(rims)):
+        back[c] = onezero(lane == turned[:, c:c + 1])
+
     def store(value):
         tend[pl.ds(tm, tm), :] = value
 
@@ -283,7 +286,7 @@
 
     def spread(c):
         rows = tend[pl.ds(base_s[c, 0], CHUNK), :].astype(jnp.bfloat16)
-        return mm(onezero(lane == turned[:, c:c + 1]), rows)
+        return mm(back[c], rows)
 
     for k, rim in enumerate(rims):
         rim[...] = rim[...] + spread(chunks + k)
@@ -384,6 +387,7 @@
             pltpu.VMEM((cols, ch), f32),
             pltpu.VMEM((tm + CHUNK, ch), f32),
             pltpu.VMEM((2 * tm + CHUNK, ch), f32),
+            pltpu.VMEM((chunks + EDGES, CHUNK, CHUNK), bf16),
             pltpu.VMEM((lon, ch), f32),
             pltpu.VMEM((lon, ch), f32),
             pltpu.VMEM((CHUNK, ch), f32),

time: 24.6 us -> 24.6 us (level)
  no operation moved by 1% of the time
where the time goes in v5:
time: 24.6 us; the launch traced here: 24.4 us
  Pallas kernels  24.2 us (98%)
    pallas_call x1, Pallas kernels, local(): pl.pallas_call(second_kernel, out_shape=jax.ShapeDtypeStruct((cols, ch),...  10.6 us
    pallas_call x1, Pallas kernels, local(): pl.pallas_call(functools.partial(first_kernel, ntx, nty), out_shape=[pltp...  9.34 us
    pallas_call x1, Pallas kernels, local(): pl.pallas_call(prepare_kernel, out_shape=[pltpu.VMEM((lon, lat, ch), f32)...  4.3 us

profile of v5, /device:TPU:0, one launch (start us, length us, event | category | flops | bytes accessed | tf_op | source)
XLA Modules:
  0.0 24.4 jit_solution(2216625994128961921)
XLA Ops:
  0.0 0.0 copy-start
  0.0 0.0 copy-start.1
  0.0 4.3 %prepare.1 = (f32[128,32,128]{2,1,0:T(8,128)S(1)}, f32[2176,128]{1,0:T(8,128)S(1)}, f32[128,128]{1,0:T(8,128)S(1)}, f32[128,128]{1,0:T(8,128)S(1)}, f32[32,128]{...) custom-call(f32[128,32,128]{2,1,0:T(8,128)} %state_hbm.1, ...), custom_call_target="tpu_custom_call" | custom-call | tf_op jit(solution)/shard_map/prepare/pallas_call | solution.py:325
  4.3 0.0 copy-done
  4.3 0.0 copy-done.1
  4.3 9.3 %first.1 = (f32[1024,128]{1,0:T(8,128)S(1)}, f32[128,128]{1,0:T(8,128)S(1)}, f32[128,128]{1,0:T(8,128)S(1)}, f32[32,128]{1,0:T(8,128)S(1)}, f32[32,128]{1,0:T(8,128)S(1)}) custom-call(f32[2176,128]{1,0:T(8,128)S(1)} %get-tuple-element.25.packed, f32[128,128]{1,0:T(8,128)S(1)} %get-tuple-element.26.edge_n, f32[128,128]{1,0:T(8,128)S(1)} %get-tuple-element.27.edge_s, ...), custom_call_target="tpu_custom_call" | custom-call | tf_op jit(solution)/shard_map/first/pallas_call | solution.py:360
  13.7 10.6 %second.1 = f32[4096,128]{1,0:T(8,128)} custom-call(f32[128,32,128]{2,1,0:T(8,128)S(1)} %get-tuple-element.24.adv, f32[2176,128]{1,0:T(8,128)S(1)} %get-tuple-element.25.packed, f32[1024,128]{1,0:T(8,128)S(1)} %get-tuple-element.31.head, f32[128,128]{1,0:T(8,128)S(1)} %get-tuple-element.32.halo_n, f32[128,128]{1,0:T(8,128)S(1)} %get-tuple-element.33.halo_s, ...), custom_call_target="tpu_custom_call" | custom-call | tf_op jit(solution)/shard_map/second/pallas_call | solution.py:381
Async XLA Ops:
  0.0 4.3 %copy-start = (bf16[128,1024]{1,0:T(8,128)(2,1)S(1)}, bf16[128,1024]{1,0:T(8,128)(2,1)}, u32[]{:S(2)}) copy-start(bf16[128,1024]{1,0:T(8,128)(2,1)} %win.3) | copy-start | bytes 786436
  0.0 4.3 %copy-start.1 = (bf16[1024,128]{1,0:T(8,128)(2,1)S(1)}, bf16[1024,128]{1,0:T(8,128)(2,1)}, u32[]{:S(2)}) copy-start(bf16[1024,128]{1,0:T(8,128)(2,1)} %wout.3) | copy-start | bytes 786436
